TPU v7x, 32 devices: a whole 2x2x4 slice. The times are simulated.
32 devices in a mesh: dp: 4 (over z), seq: 2 (over y), mp: 4 (over x, core).
Axes of the slice: x: 2, y: 2, z: 4, core: 2. Of those that a mesh axis runs over, the one named last changes fastest.
Arguments:
- hidden_in: bfloat16 [4, 1024, 768], P('dp', 'seq', 'mp'), may hold values from -6 to 6
- cotangent: bfloat16 [4, 1024, 768], P('dp', 'seq', 'mp'), may hold values from -6 to 6
- attention_gain: float32 [768], replicated, may hold values from 0.1 to 1.9
- feedforward_gain: float32 [768], replicated, may hold values from 0.1 to 1.9
- qkv_weight: bfloat16 [768, 3, 768], P(None, None, 'mp'), may hold values from -0.21875 to 0.21875
- attention_out: bfloat16 [768, 768], P('mp'), may hold values from -0.75 to 0.75
- geglu_in: bfloat16 [768, 2, 1152], P(None, None, 'mp'), may hold values from -0.21875 to 0.21875
- geglu_out: bfloat16 [1152, 768], P('mp'), may hold values from -0.1875 to 0.1875
Outputs:
- layer_out: float32 [4, 1024, 768], P('dp', 'seq', 'mp')
- grad_input: float32 [4, 1024, 768], P('dp', 'seq', 'mp')
- grad_qkv: float32 [768, 3, 768], P(None, None, 'mp')
- grad_attention_out: float32 [768, 768], P('mp')
- grad_geglu_in: float32 [768, 2, 1152], P(None, None, 'mp')
- grad_geglu_out: float32 [1152, 768], P('mp')
- grad_attention_gain: float32 [768], P('mp')
- grad_feedforward_gain: float32 [768], P('mp')
All inputs are finite; a program needn't handle non-finite values.
Results may differ from a plain program's by a relative error of at most 0.018.
Values may be sent and summed in bfloat16 or wider, within the bound.
No kernel may reach another device: no remote copies, remote signals or barrier semaphores. Data moves between devices by JAX's collectives and lax.ppermute only.
A program may use at most 64 MiB of HBM per device.

v0:
```python
import math
import jax
import jax.numpy as jnp
from jax import lax
from jax.sharding import PartitionSpec as P

HEAD = 64
HALF = 64


def with_halo(block, sides, width):
    for axis, dim in sides:
        count = lax.axis_size(axis)
        forward = [(i, i + 1) for i in range(count - 1)]
        backward = [(target, source) for source, target in forward]
        low = lax.ppermute(
            lax.slice_in_dim(block, block.shape[dim] - width, None, axis=dim), axis, forward
        )
        high = lax.ppermute(lax.slice_in_dim(block, 0, width, axis=dim), axis, backward)
        block = jnp.concatenate([low, block, high], axis=dim)
    return block


def normalize(rows):
    center = rows - jnp.mean(rows, axis=-1, keepdims=True)
    inverse = lax.rsqrt(jnp.mean(center * center, axis=-1, keepdims=True) + 1e-05)
    return (center * inverse, inverse)


def frequencies(positions):
    inverse_freq = jnp.exp(
        jnp.arange(HEAD // 2).astype(jnp.float32) * (-2.0 * math.log(10000.0) / HEAD)
    )
    angles = positions[:, None] * inverse_freq[None, :]
    angles = jnp.concatenate([angles, angles], axis=-1)
    return (jnp.cos(angles), jnp.sin(angles))


def rotate(tensor, cosine, sine):
    halfway = HEAD // 2
    turned = jnp.concatenate([-tensor[..., halfway:], tensor[..., :halfway]], axis=-1)
    return tensor * cosine[:, None, :] + turned * sine[:, None, :]


def gelu_exact(value):
    return 0.5 * value * (1.0 + lax.erf(value * 0.7071067811865476))


def gelu_slope(value):
    return (
        0.5 * (1.0 + lax.erf(value * 0.7071067811865476))
        + value * jnp.exp(-0.5 * value * value) * 0.3989422804014327
    )


def windows(wide, tile):
    count = (wide.shape[1] - tile) // tile
    shape = (wide.shape[0], count, tile) + wide.shape[2:]
    lower = wide[:, : count * tile].reshape(shape)
    upper = wide[:, tile:].reshape(shape)
    return jnp.concatenate([lower, upper], axis=2)


def unwindow(grads, tile):
    rest = grads.shape[3:]
    shape = (grads.shape[0], grads.shape[1] * tile) + rest
    lower = grads[:, :, :tile].reshape(shape)
    upper = grads[:, :, tile:].reshape(shape)
    others = ((0, 0),) * len(rest)
    return jnp.pad(lower, ((0, 0), (0, tile)) + others) + jnp.pad(
        upper, ((0, 0), (tile, 0)) + others
    )


def band_mask(base, count, tile, total_length):
    query_off = jnp.arange(tile, dtype=jnp.int32)
    key_off = jnp.arange(2 * tile, dtype=jnp.int32) - HALF
    near = jnp.abs(query_off[:, None] - key_off[None, :]) <= HALF
    key_pos = (
        base
        - HALF
        + jnp.arange(count, dtype=jnp.int32)[:, None] * tile
        + jnp.arange(2 * tile, dtype=jnp.int32)[None, :]
    )
    inside = (key_pos >= 0) & (key_pos < total_length)
    return near[None] & inside[:, None, :]


def attend(queries, keys_wide, values_wide, allowed):
    batch, length, heads, size = queries.shape
    tile = 2 * HALF
    count = length // tile
    query_tiles = queries.reshape(batch, count, tile, heads, size)
    key_tiles = windows(keys_wide, tile)
    value_tiles = windows(values_wide, tile)
    scores = jnp.einsum(
        "snqhd,snkhd->snhqk", query_tiles, key_tiles, preferred_element_type=jnp.float32
    ) * HEAD ** (-0.5)
    scores = jnp.where(allowed[None, :, None], scores, -1e30)
    top = jnp.max(scores, axis=-1, keepdims=True)
    log_total = top + jnp.log(jnp.sum(jnp.exp(scores - top), axis=-1, keepdims=True))
    weights = jnp.exp(scores - log_total).astype(jnp.bfloat16)
    mixed = jnp.einsum(
        "snhqk,snkhd->snqhd", weights, value_tiles, preferred_element_type=jnp.float32
    ).astype(jnp.bfloat16)
    return (mixed.reshape(batch, length, heads, size), log_total)


def attend_back(queries, keys_wide, values_wide, allowed, log_total, mixed, grad_mixed):
    batch, length, heads, size = queries.shape
    tile = 2 * HALF
    count = length // tile
    query_tiles = queries.reshape(batch, count, tile, heads, size)
    key_tiles = windows(keys_wide, tile)
    value_tiles = windows(values_wide, tile)
    grad_tiles = grad_mixed.reshape(batch, count, tile, heads, size)
    again = jnp.einsum(
        "snqhd,snkhd->snhqk", query_tiles, key_tiles, preferred_element_type=jnp.float32
    ) * HEAD ** (-0.5)
    again = jnp.where(allowed[None, :, None], again, -1e30)
    probs = jnp.exp(again - log_total)
    delta = jnp.sum(grad_mixed.astype(jnp.float32) * mixed.astype(jnp.float32), axis=-1)
    delta = jnp.transpose(delta.reshape(batch, count, tile, heads), (0, 1, 3, 2))
    grad_value_tiles = jnp.einsum(
        "snhqk,snqhd->snkhd",
        probs.astype(jnp.bfloat16),
        grad_tiles,
        preferred_element_type=jnp.float32,
    )
    grad_probs = jnp.einsum(
        "snqhd,snkhd->snhqk", grad_tiles, value_tiles, preferred_element_type=jnp.float32
    )
    grad_scores = (probs * (grad_probs - delta[..., None]) * HEAD ** (-0.5)).astype(jnp.bfloat16)
    grad_queries = jnp.einsum(
        "snhqk,snkhd->snqhd", grad_scores, key_tiles, preferred_element_type=jnp.float32
    )
    grad_key_tiles = jnp.einsum(
        "snhqk,snqhd->snkhd", grad_scores, query_tiles, preferred_element_type=jnp.float32
    )
    return (
        grad_queries.reshape(batch, length, heads, size),
        unwindow(grad_key_tiles, tile),
        unwindow(grad_value_tiles, tile),
    )


def edge_rims(grad_packed, length):
    return jnp.concatenate([grad_packed[:, :HALF], grad_packed[:, HALF + length :]], axis=1)


def fold_rims(grad_packed, returned, length):
    lower_add = jnp.pad(returned[:, :HALF], ((0, 0), (0, length - HALF), (0, 0)))
    upper_add = jnp.pad(returned[:, 3 * HALF :], ((0, 0), (length - HALF, 0), (0, 0)))
    return grad_packed[:, HALF : HALF + length] + lower_add + upper_add


def body(
    hidden_in,
    cotangent,
    attention_gain,
    feedforward_gain,
    qkv_weight,
    attention_out,
    geglu_in,
    geglu_out,
):
    batch, length, share = hidden_in.shape
    width = share * lax.axis_size("mp")
    offset = lax.axis_index("mp") * share
    columns = qkv_weight.shape[2]
    heads = columns // HEAD
    span = length + 2 * HALF
    inputs_full, upstream_full = (
        lax.all_gather(hidden_in, "mp", axis=2, tiled=True),
        lax.all_gather(cotangent, "mp", axis=2, tiled=True),
    )
    normed_one, inverse_one = normalize(inputs_full.astype(jnp.float32))
    fed_one = (normed_one * attention_gain).astype(jnp.bfloat16)
    projected = jnp.einsum("std,dch->stch", fed_one, qkv_weight, preferred_element_type=jnp.float32)
    block_index = lax.axis_index("seq")
    total_length = length * lax.axis_size("seq")
    query_pos = block_index * length + jnp.arange(length, dtype=jnp.int32)
    cosine, sine = frequencies(query_pos.astype(jnp.float32))
    queries = rotate(projected[:, :, 0].reshape(batch, length, heads, HEAD), cosine, sine).astype(
        jnp.bfloat16
    )
    keys_own = rotate(projected[:, :, 1].reshape(batch, length, heads, HEAD), cosine, sine).astype(
        jnp.bfloat16
    )
    values_own = projected[:, :, 2].astype(jnp.bfloat16)
    packed = jnp.concatenate([keys_own.reshape(batch, length, columns), values_own], axis=2)
    widened = with_halo(packed, (("seq", 1),), HALF)
    keys_wide = widened[:, :, :columns].reshape(batch, span, heads, HEAD)
    values_wide = widened[:, :, columns:].reshape(batch, span, heads, HEAD)
    allowed = band_mask(block_index * length, length // (2 * HALF), 2 * HALF, total_length)
    mixed, log_total = attend(queries, keys_wide, values_wide, allowed)
    joined = mixed.reshape(batch, length, columns)
    attn_terms = jnp.einsum(
        "sqh,hd->sqd", joined, attention_out, preferred_element_type=jnp.float32
    )
    middle = hidden_in.astype(jnp.float32) + lax.psum_scatter(
        attn_terms, "mp", scatter_dimension=2, tiled=True
    )
    middle_full = lax.all_gather(middle, "mp", axis=2, tiled=True)
    normed_two, inverse_two = normalize(middle_full)
    fed_two = (normed_two * feedforward_gain).astype(jnp.bfloat16)
    lifted = jnp.einsum("std,dcf->stcf", fed_two, geglu_in, preferred_element_type=jnp.float32)
    linear = lifted[:, :, 0]
    gating = lifted[:, :, 1]
    activated = gelu_exact(linear)
    product = (activated * gating).astype(jnp.bfloat16)
    mlp_terms = jnp.einsum("stf,fd->std", product, geglu_out, preferred_element_type=jnp.float32)
    layer_out = middle + lax.psum_scatter(
        mlp_terms.astype(jnp.bfloat16), "mp", scatter_dimension=2, tiled=True
    ).astype(jnp.float32)
    grad_geglu_out = jnp.einsum(
        "stf,std->fd", product, upstream_full, preferred_element_type=jnp.float32
    )
    grad_product = jnp.einsum(
        "std,fd->stf", upstream_full, geglu_out, preferred_element_type=jnp.float32
    )
    grad_linear = grad_product * gating * gelu_slope(linear)
    grad_gating = grad_product * activated
    grad_lifted = jnp.stack([grad_linear, grad_gating], axis=2).astype(jnp.bfloat16)
    grad_geglu_in = jnp.einsum(
        "std,stcf->dcf", fed_two, grad_lifted, preferred_element_type=jnp.float32
    )
    fed_terms = jnp.einsum(
        "stcf,dcf->std", grad_lifted, geglu_in, preferred_element_type=jnp.float32
    )
    grad_fed_two = lax.psum_scatter(fed_terms, "mp", scatter_dimension=2, tiled=True)
    normed_two_own = lax.dynamic_slice_in_dim(normed_two, offset, share, 2)
    gain_two_own = lax.dynamic_slice_in_dim(feedforward_gain, offset, share, 0)
    grad_ff_gain = jnp.sum(grad_fed_two * normed_two_own, axis=(0, 1))
    dhat_two = grad_fed_two * gain_two_own
    first_two, second_two = lax.psum(
        (
            jnp.sum(dhat_two, axis=-1, keepdims=True),
            jnp.sum(dhat_two * normed_two_own, axis=-1, keepdims=True),
        ),
        "mp",
    )
    grad_middle = cotangent.astype(jnp.float32) + inverse_two * (
        dhat_two - first_two / width - normed_two_own * (second_two / width)
    )
    grad_middle_full = lax.all_gather(grad_middle.astype(jnp.bfloat16), "mp", axis=2, tiled=True)
    grad_attention_out = jnp.einsum(
        "sqh,sqd->hd", joined, grad_middle_full, preferred_element_type=jnp.float32
    )
    grad_mixed = jnp.einsum(
        "sqd,hd->sqh", grad_middle_full, attention_out, preferred_element_type=jnp.float32
    ).astype(jnp.bfloat16)
    grad_mixed = grad_mixed.reshape(batch, length, heads, HEAD)
    grad_queries, grad_keys_wide, grad_values_wide = attend_back(
        queries, keys_wide, values_wide, allowed, log_total, mixed, grad_mixed
    )
    grad_packed = jnp.concatenate(
        [
            grad_keys_wide.reshape(batch, span, columns),
            grad_values_wide.reshape(batch, span, columns),
        ],
        axis=2,
    )
    returned = with_halo(
        edge_rims(grad_packed, length).astype(jnp.bfloat16), (("seq", 1),), HALF
    ).astype(jnp.float32)
    grad_own = fold_rims(grad_packed, returned, length)
    grad_keys = rotate(grad_own[:, :, :columns].reshape(batch, length, heads, HEAD), cosine, -sine)
    grad_queries = rotate(grad_queries, cosine, -sine)
    grad_values = grad_own[:, :, columns:].reshape(batch, length, heads, HEAD)
    grad_projected = (
        jnp.stack([grad_queries, grad_keys, grad_values], axis=2)
        .reshape(batch, length, 3, columns)
        .astype(jnp.bfloat16)
    )
    grad_qkv = jnp.einsum(
        "std,stch->dch", fed_one, grad_projected, preferred_element_type=jnp.float32
    )
    one_terms = jnp.einsum(
        "stch,dch->std", grad_projected, qkv_weight, preferred_element_type=jnp.float32
    )
    grad_fed_one = lax.psum_scatter(
        one_terms.astype(jnp.bfloat16), "mp", scatter_dimension=2, tiled=True
    ).astype(jnp.float32)
    normed_one_own = lax.dynamic_slice_in_dim(normed_one, offset, share, 2)
    gain_one_own = lax.dynamic_slice_in_dim(attention_gain, offset, share, 0)
    grad_attn_gain = jnp.sum(grad_fed_one * normed_one_own, axis=(0, 1))
    dhat_one = grad_fed_one * gain_one_own
    first_one, second_one = lax.psum(
        (
            jnp.sum(dhat_one, axis=-1, keepdims=True),
            jnp.sum(dhat_one * normed_one_own, axis=-1, keepdims=True),
        ),
        "mp",
    )
    grad_input = grad_middle + inverse_one * (
        dhat_one - first_one / width - normed_one_own * (second_one / width)
    )
    local_grads = (
        grad_qkv,
        grad_attention_out,
        grad_geglu_in,
        grad_geglu_out,
        grad_attn_gain,
        grad_ff_gain,
    )
    summed = lax.psum(
        (
            local_grads[0],
            local_grads[1],
            local_grads[2],
            local_grads[3],
            local_grads[4],
            local_grads[5],
        ),
        ("dp", "seq"),
    )
    return (layer_out, grad_input, summed[0], summed[1], summed[2], summed[3], summed[4], summed[5])


def solution(mesh):
    in_specs = (
        P("dp", "seq", "mp"),
        P("dp", "seq", "mp"),
        P(),
        P(),
        P(None, None, "mp"),
        P("mp", None),
        P(None, None, "mp"),
        P("mp", None),
    )
    out_specs = (
        P("dp", "seq", "mp"),
        P("dp", "seq", "mp"),
        P(None, None, "mp"),
        P("mp", None),
        P(None, None, "mp"),
        P("mp", None),
        P("mp"),
        P("mp"),
    )
    return jax.shard_map(body, mesh=mesh, in_specs=in_specs, out_specs=out_specs, check_vma=False)
```

profile of v0, /device:TPU:0, one launch (start us, length us, event | category | flops | bytes accessed | tf_op | source)
XLA Modules:
  0.0 433.2 jit_solution(13001490404904794870)
XLA Ops:
  7.3 10.4 %all_gather.12 = bf16[1,512,768]{1,2,0:T(8,128)(2,1)S(1)} all-gather(bf16[1,512,192]{1,2,0:T(8,128)(2,1)} %param.8), channel_id=1, replica_groups=mesh['dp'=4,'seq'=2,'mp'=4] {'mp'}, dimensions={2}, use_global_device_ids=true | all-gather | bytes 983040 | tf_op jit(solution)/shard_map/all_gather | solution.py:174
  22.8 3.4 collective-permute-start
  27.8 1.7 fusion.81
  37.7 2.7 copy.56
  42.3 43.4 %all-reduce.16.cloned.1.call-done = f32[1,512,768]{1,0,2:T(1,128)} async-done(((f32[1,512,768]{1,0,2:T(1,128)}), f32[1,512,768]{1,0,2:T(1,128)}) %all-reduce.16.cloned.1.call-update) | async-done | bytes 1572880
  85.7 2.1 dynamic-slice_add_fusion
  87.9 8.6 %all_gather.14 = bf16[1,512,768]{1,2,0:T(8,128)(2,1)} all-gather(bf16[1,512,192]{1,2,0:T(8,128)(2,1)S(1)} %copy-done.12), channel_id=1, replica_groups=mesh['dp'=4,'seq'=2,'mp'=4] {'mp'}, dimensions={2}, use_global_device_ids=true | all-gather | bytes 983040 | tf_op jit(solution)/shard_map/all_gather | solution.py:175
  96.5 11.2 %all-gather.2.cloned.1.call-done = f32[1,512,768]{1,0,2:T(1,128)} async-done(((f32[1,512,192]{1,0,2:T(1,128)}), f32[1,512,768]{1,0,2:T(1,128)}) %all-gather.2.cloned.1.call-update) | async-done | bytes 1572880 | tf_op jit(solution)/shard_map/all_gather | solution.py:204
  107.7 2.4 reduce_sum.111
  115.8 2.0 convolution_bitcast_fusion
  117.8 4.8 %copy.60 = f32[1,512,768]{1,0,2:T(1,128)} copy(f32[1,512,768]{2,1,0:T(8,128)} %convolution_bitcast_fusion) | data formatting | bytes 3145728 | tf_op jit(solution)/shard_map/stcf,dcf->std/dot_general | solution.py:228
  123.6 2.9 fusion.6
  126.6 4.8 %copy.86 = bf16[1,512,768]{1,0,2:T(2,128)(2,1)} copy(bf16[1,512,768]{2,1,0:T(8,128)(2,1)} %fusion.6) | data formatting | bytes 1572864
  131.3 2.5 copy.151
  133.9 31.7 %all-reduce.18.cloned.1.call-done = f32[1,512,768]{1,0,2:T(1,128)} async-done(((f32[1,512,768]{1,0,2:T(1,128)}), f32[1,512,768]{1,0,2:T(1,128)}) %all-reduce.18.cloned.1.call-update) | async-done | bytes 1572880
  167.8 6.0 %all-reduce.11 = (f32[1,512,1]{1,2,0:T(1,128)S(1)}, f32[1,512,1]{1,2,0:T(1,128)S(1)}) all-reduce(f32[1,512,1]{1,2,0:T(1,128)S(1)} %bitcast.303, f32[1,512,1]{1,2,0:T(1,128)S(1)} %bitcast.304), channel_id=1, replica_groups=mesh['dp'=4,'seq'=2,'mp'=4] {'mp'}, use_global_device_ids=true, to_apply=%region_12.13 | all-reduce | flops 1024 | bytes 8192 | tf_op jit(solution)/shard_map/psum | solution.py:236
  175.0 8.3 %all_gather.15 = bf16[1,512,768]{1,2,0:T(8,128)(2,1)S(1)} all-gather(bf16[1,512,192]{1,2,0:T(8,128)(2,1)S(1)} %fusion.98), channel_id=1, replica_groups=mesh['dp'=4,'seq'=2,'mp'=4] {'mp'}, dimensions={2}, use_global_device_ids=true | all-gather | bytes 983040 | tf_op jit(solution)/shard_map/all_gather | solution.py:246
  187.0 2.1 convolution_bitcast_fusion.3
  193.4 3.4 collective-permute-start.2
  199.4 4.1 collective-permute-done.3
  206.1 1.7 fusion.5
  207.9 4.8 %copy.88 = bf16[1,512,768]{1,0,2:T(2,128)(2,1)} copy(bf16[1,512,768]{2,1,0:T(8,128)(2,1)} %fusion.5) | data formatting | bytes 1572864
  212.6 2.5 copy.150
  215.2 2.9 fusion.16
  218.1 1.9 fusion.48
  221.4 2.0 fusion.76
  227.1 10.6 %reduce-scatter.9.cloned.1.call-done = bf16[192,512]{1,0:T(8,128)(2,1)} async-done(((bf16[768,512]{1,0:T(8,128)(2,1)}), bf16[192,512]{1,0:T(8,128)(2,1)}) %reduce-scatter.9.cloned.1.call-update) | async-done | bytes 196624
  240.0 22.6 %all-reduce.8 = (f32[192]{0:T(256)}, f32[192]{0:T(256)}) all-reduce(f32[192]{0:T(256)S(1)} %get-tuple-element.34, f32[192]{0:T(256)S(1)} %get-tuple-element.32), channel_id=1, replica_groups=mesh['dp'=4,'seq'=2,'mp'=4] {'dp','seq'}, use_global_device_ids=true, to_apply=%region_24.25 | all-reduce | flops 384 | bytes 3072 | tf_op jit(solution)/shard_map/psum | solution.py:307
  262.6 6.0 %all-reduce.10 = (f32[1,512,1]{1,2,0:T(1,128)S(1)}, f32[1,512,1]{1,2,0:T(1,128)S(1)}) all-reduce(f32[1,512,1]{1,2,0:T(1,128)S(1)} %bitcast.301, f32[1,512,1]{1,2,0:T(1,128)S(1)} %bitcast.302), channel_id=1, replica_groups=mesh['dp'=4,'seq'=2,'mp'=4] {'mp'}, use_global_device_ids=true, to_apply=%region_18.19 | all-reduce | flops 1024 | bytes 8192 | tf_op jit(solution)/shard_map/psum | solution.py:289
  268.7 2.0 fusion.35
  270.7 149.2 %all-reduce.20.cloned.1.call-done = (f32[768,3,192]{0,2,1:T(8,128)}, f32[192,768]{1,0:T(8,128)}, f32[768,2,288]{0,2,1:T(8,128)}, f32[288,768]{1,0:T(8,128)}) async-done(((f32[768,3,192]{0,2,1:T(8,128)}, f32[192,768]{1,0:T(8,128)}, f32[768,2,288]{0,2,1:T(8,128)}, f32[288,768]{1,0:T(8,128)}), (f32[768,3,192]{0,2,1:T(8,128)}, f32[192,768]{1,0:T(8,128)}, f32[768,2,288]{0,2,1:T(8,128)}, ...) | async-done | bytes 5013520 | tf_op jit(solution)/shard_map/psum | solution.py:307
  419.9 2.9 copy.158
  (219 shorter events, 49.8 us)
Async XLA Ops:
  7.2 10.9 %copy-start = (bf16[768,3,192]{0,2,1:T(8,128)(2,1)S(1)}, bf16[768,3,192]{0,2,1:T(8,128)(2,1)}, u32[]{:S(2)}) copy-start(bf16[768,3,192]{0,2,1:T(8,128)(2,1)} %param.12) | copy-start | bytes 2654212
  7.2 10.9 %copy-start.47 = (f32[768]{0:T(1024)S(1)}, f32[768]{0:T(1024)}, u32[]{:S(2)}) copy-start(f32[768]{0:T(1024)} %param.10) | copy-start | bytes 9220
  7.2 78.5 %all-reduce.16.cloned.1.call-start = ((), (), s32[]{:S(2)}) async-start(), calls=%async_computation.5 | async-start | bytes 3145728
  20.9 1.9 copy-start.18
  22.8 9.8 %collective-permute-start = (bf16[1,64,384]{1,2,0:T(8,128)(2,1)}, bf16[1,64,384]{1,2,0:T(8,128)(2,1)S(1)}, u32[]{:S(2)}, u32[]{:S(2)}) collective-permute-start(bf16[1,64,384]{1,2,0:T(8,128)(2,1)} %get-tuple-element.71), channel_id=1, source_target_pairs={{0,4},{1,5},{2,6},{3,7},{8,12},{9,13},{10,14},{11,15},{16,20},{17,... | collective-permute-start | bytes 147464 | tf_op jit(solution)/shard_map/ppermute | solution.py:16
  26.2 6.8 %collective-permute-start.1 = (bf16[1,64,384]{1,2,0:T(8,128)(2,1)S(1)}, bf16[1,64,384]{1,2,0:T(8,128)(2,1)}, u32[]{:S(2)}, u32[]{:S(2)}) collective-permute-start(bf16[1,64,384]{1,2,0:T(8,128)(2,1)S(1)} %get-tuple-element.72), channel_id=1, source_target_pairs={{4,0},{5,1},{6,2},{7,3},{12,8},{13,9},{14,10},{15,11},{20,16},{21,... | collective-permute-start | bytes 147464 | tf_op jit(solution)/shard_map/ppermute | solution.py:19
  32.6 1.9 copy-start.24
  40.4 45.3 %copy-start.35 = (bf16[1,512,192]{1,2,0:T(8,128)(2,1)S(1)}, bf16[1,512,192]{1,2,0:T(8,128)(2,1)}, u32[]{:S(2)}) copy-start(bf16[1,512,192]{1,2,0:T(8,128)(2,1)} %param.8) | copy-start | bytes 589828
  40.4 47.5 %copy-start.12 = (bf16[1,512,192]{1,2,0:T(8,128)(2,1)S(1)}, bf16[1,512,192]{1,2,0:T(8,128)(2,1)}, u32[]{:S(2)}) copy-start(bf16[1,512,192]{1,2,0:T(8,128)(2,1)} %param.9) | copy-start | bytes 589828
  40.5 67.3 %all-gather.2.cloned.1.call-start = ((), (), s32[]{:S(2)}) async-start(), calls=%async_computation.2 | async-start | bytes 1966080 | tf_op jit(solution)/shard_map/all_gather | solution.py:204
  87.9 77.7 %all-reduce.18.cloned.1.call-start = ((), (), s32[]{:S(2)}) async-start(), calls=%async_computation.6 | async-start | bytes 3145728
  107.7 2.4 copy-start.3
  122.6 102.3 %reduce-scatter.7.cloned.1.call-start = ((), (), s32[]{:S(2)}) async-start(), calls=%async_computation.3 | async-start | bytes 983040
  133.8 40.0 %copy-start.13 = (bf16[1,512,192]{1,2,0:T(8,128)(2,1)S(1)}, bf16[1,512,192]{1,2,0:T(8,128)(2,1)}, u32[]{:S(2)}) copy-start(bf16[1,512,192]{1,2,0:T(8,128)(2,1)} %param.9) | copy-start | bytes 589828
  133.9 103.9 %reduce-scatter.9.cloned.1.call-start = ((), (), s32[]{:S(2)}) async-start(), calls=%async_computation.4 | async-start | bytes 983040
  173.8 10.4 %copy-start.21 = (bf16[192,768]{1,0:T(8,128)(2,1)S(1)}, bf16[192,768]{1,0:T(8,128)(2,1)}, u32[]{:S(2)}) copy-start(bf16[192,768]{1,0:T(8,128)(2,1)} %param.13) | copy-start | bytes 884740
  185.3 3.8 copy-start.26
  187.0 2.2 copy-start.2
  187.0 2.2 copy-start.32
  187.0 2.2 copy-start.34
  193.4 5.9 %collective-permute-start.2 = (bf16[1,64,384]{1,2,0:T(8,128)(2,1)S(1)}, bf16[1,64,384]{1,2,0:T(8,128)(2,1)S(1)}, u32[]{:S(2)}, u32[]{:S(2)}) collective-permute-start(bf16[1,64,384]{1,2,0:T(8,128)(2,1)S(1)} %get-tuple-element.53), channel_id=1, source_target_pairs={{0,4},{1,5},{2,6},{3,7},{8,12},{9,13},{10,14},{11,15},{16,20},{17,... | collective-permute-start | bytes 147464 | tf_op jit(solution)/shard_map/ppermute | solution.py:16
  196.8 6.7 %collective-permute-start.3 = (bf16[1,64,384]{1,2,0:T(8,128)(2,1)S(1)}, bf16[1,64,384]{1,2,0:T(8,128)(2,1)S(1)}, u32[]{:S(2)}, u32[]{:S(2)}) collective-permute-start(bf16[1,64,384]{1,2,0:T(8,128)(2,1)S(1)} %get-tuple-element.54), channel_id=1, source_target_pairs={{4,0},{5,1},{6,2},{7,3},{12,8},{13,9},{14,10},{15,11},{20,16},{21,... | collective-permute-start | bytes 147464 | tf_op jit(solution)/shard_map/ppermute | solution.py:19
  215.1 204.8 %all-reduce.20.cloned.1.call-start = ((), (), s32[]{:S(2)}) async-start(), calls=%async_computation.7 | async-start | bytes 10027008 | tf_op jit(solution)/shard_map/psum | solution.py:307
  215.2 2.9 copy-start.43
  215.2 2.9 copy-start.45
  218.1 2.0 copy-start.6
  218.1 2.0 copy-start.16
  224.9 43.8 %copy-start.8 = (f32[1,512,192]{1,0,2:T(1,128)S(1)}, f32[1,512,192]{1,0,2:T(1,128)}, u32[]{:S(2)}) copy-start(f32[1,512,192]{1,0,2:T(1,128)} %copy-done.7) | copy-start | bytes 1179652
  224.9 43.8 %copy-start.14 = (bf16[1,512,192]{1,2,0:T(8,128)(2,1)S(1)}, bf16[1,512,192]{1,2,0:T(8,128)(2,1)}, u32[]{:S(2)}) copy-start(bf16[1,512,192]{1,2,0:T(8,128)(2,1)} %param.9) | copy-start | bytes 589828
  419.9 3.0 copy-start.40
  419.9 3.8 copy-start.11
  423.7 1.8 copy-start.23
  (28 other events, 27.4 us)
Sparse Core Ops, SparseCore 0:
  40.6 45.0 all-reduce.15
  88.0 19.6 all-gather.1
  122.7 42.8 all-reduce.17
  168.0 23.2 reduce-scatter.6
  215.3 22.4 reduce-scatter.8
  242.1 177.7 all-reduce.19
where the time goes:
time: 434 us; the launch traced here: 433 us
  waiting for transfers between devices  251 us (58%)
  blocking collectives  61.9 us (14%)
  local copies, waits for them, and re-layouts  47.5 us (11%)
  other arithmetic  25.6 us (6%)
  matrix products  21.8 us (5%)
  between operations  15.6 us (4%)
  starting transfers between devices  9.63 us (2%)
    psum x1, waiting for transfers between devices, body(): lax.psum((local_grads[0], local_grads[1], local_grads[2], local_grads[3],...  149 us
    unnamed x10, waiting for transfers between devices  85.8 us
    unnamed x117, local copies, waits for them, and re-layouts  34.8 us
    psum x1, blocking collectives, body(): lax.psum((local_grads[0], local_grads[1], local_grads[2], local_grads[3],...  22.6 us
    all_gather x1, waiting for transfers between devices, body(): middle_full = lax.all_gather(middle, 'mp', axis=2, tiled=True)  11.2 us
    all_gather x1, blocking collectives, body(): lax.all_gather(hidden_in, 'mp', axis=2, tiled=True)  10.4 us
  transfers between devices with their start and end apart: 10, of which 8 were waited for; matrix products, arithmetic and copies ran while one was open for 13% of the time, Pallas kernels for 0%

commit v1 on v0

--- a/solution.py
+++ b/solution.py
@@ -305,15 +305,18 @@
         grad_ff_gain,
     )
     summed = lax.psum(
-        (
-            local_grads[0],
-            local_grads[1],
-            local_grads[2],
-            local_grads[3],
-            local_grads[4],
-            local_grads[5],
+        lax.psum(
+            (
+                local_grads[0],
+                local_grads[1],
+                local_grads[2],
+                local_grads[3],
+                local_grads[4],
+                local_grads[5],
+            ),
+            "dp",
         ),
-        ("dp", "seq"),
+        "seq",
     )
     return (layer_out, grad_input, summed[0], summed[1], summed[2], summed[3], summed[4], summed[5])
 

time: 434 us -> 580 us (1.34)
  waiting for transfers between devices: 251 us -> 405 us
    psum x0 -> x1, waiting for transfers between devices: none -> 101 us  [body(): lax.psum(lax.psum((local_grads[0], local_grads[1], local_grads[2], local_...]
    unnamed x10 -> x11, waiting for transfers between devices: 85.8 us -> 125 us
    psum x1, waiting for transfers between devices: 149 us -> 160 us  [body(): lax.psum((local_grads[0], local_grads[1], local_grads[2], local_grads[3],...]
    psum x1, blocking collectives: 22.6 us -> 11.7 us  [body(): lax.psum((local_grads[0], local_grads[1], local_grads[2], local_grads[3],...]
    unnamed x117 -> x109, local copies, waits for them, and re-layouts: 34.8 us -> 33.3 us
  transfers between devices with their start and end apart: 10 -> 11, of which waited for: 8 -> 10; matrix products, arithmetic and copies ran while one was open for 13% -> 6% of each run, Pallas kernels for 0% -> 0%
where the time goes in v1:
time: 580 us; the launch traced here: 579 us
  waiting for transfers between devices  405 us (70%)
  blocking collectives  56.7 us (10%)
  local copies, waits for them, and re-layouts  45.1 us (8%)
  other arithmetic  23.3 us (4%)
  matrix products  22.9 us (4%)
  between operations  15.7 us (3%)
  starting transfers between devices  10.3 us (2%)
    psum x1, waiting for transfers between devices, body(): lax.psum((local_grads[0], local_grads[1], local_grads[2], local_grads[3],...  160 us
    unnamed x11, waiting for transfers between devices  125 us
    psum x1, waiting for transfers between devices, body(): lax.psum(lax.psum((local_grads[0], local_grads[1], local_grads[2], local_...  101 us
    unnamed x109, local copies, waits for them, and re-layouts  33.3 us
    psum x1, blocking collectives, body(): lax.psum((local_grads[0], local_grads[1], local_grads[2], local_grads[3],...  11.7 us
  transfers between devices with their start and end apart: 11, of which 10 were waited for; matrix products, arithmetic and copies ran while one was open for 6% of the time, Pallas kernels for 0%

profile of v1, /device:TPU:0, one launch (start us, length us, event | category | flops | bytes accessed | tf_op | source)
XLA Modules:
  0.0 579.3 jit_solution(18368713442279737928)
XLA Ops:
  7.3 10.4 %all_gather.12 = bf16[1,512,768]{1,2,0:T(8,128)(2,1)S(1)} all-gather(bf16[1,512,192]{1,2,0:T(8,128)(2,1)} %param.8), channel_id=1, replica_groups=mesh['dp'=4,'seq'=2,'mp'=4] {'mp'}, dimensions={2}, use_global_device_ids=true | all-gather | bytes 983040 | tf_op jit(solution)/shard_map/all_gather | solution.py:174
  22.8 4.1 collective-permute-start
  30.1 3.8 collective-permute-done.1
  38.6 2.7 copy.56
  43.2 41.0 %all-reduce.19.cloned.1.call-done = f32[1,512,768]{1,0,2:T(1,128)} async-done(((f32[1,512,768]{1,0,2:T(1,128)}), f32[1,512,768]{1,0,2:T(1,128)}) %all-reduce.19.cloned.1.call-update) | async-done | bytes 1572880
  84.2 2.1 dynamic-slice_add_fusion
  86.5 8.6 %all_gather.14 = bf16[1,512,768]{1,2,0:T(8,128)(2,1)} all-gather(bf16[1,512,192]{1,2,0:T(8,128)(2,1)S(1)} %copy-done.10), channel_id=1, replica_groups=mesh['dp'=4,'seq'=2,'mp'=4] {'mp'}, dimensions={2}, use_global_device_ids=true | all-gather | bytes 983040 | tf_op jit(solution)/shard_map/all_gather | solution.py:175
  95.1 11.2 %all-gather.2.cloned.1.call-done = f32[1,512,768]{1,0,2:T(1,128)} async-done(((f32[1,512,192]{1,0,2:T(1,128)}), f32[1,512,768]{1,0,2:T(1,128)}) %all-gather.2.cloned.1.call-update) | async-done | bytes 1572880 | tf_op jit(solution)/shard_map/all_gather | solution.py:204
  106.3 2.4 reduce_sum.111
  116.3 4.8 copy.60
  122.2 2.9 fusion.16
  127.0 37.1 %all-reduce.21.cloned.1.call-done = f32[1,512,768]{1,0,2:T(1,128)} async-done(((f32[1,512,768]{1,0,2:T(1,128)}), f32[1,512,768]{1,0,2:T(1,128)}) %all-reduce.21.cloned.1.call-update) | async-done | bytes 1572880
  166.4 6.0 %all-reduce.9 = (f32[1,512,1]{1,2,0:T(1,128)S(1)}, f32[1,512,1]{1,2,0:T(1,128)S(1)}) all-reduce(f32[1,512,1]{1,2,0:T(1,128)S(1)} %bitcast.303, f32[1,512,1]{1,2,0:T(1,128)S(1)} %bitcast.304), channel_id=1, replica_groups=mesh['dp'=4,'seq'=2,'mp'=4] {'mp'}, use_global_device_ids=true, to_apply=%region_12.13 | all-reduce | flops 1024 | bytes 8192 | tf_op jit(solution)/shard_map/psum | solution.py:236
  173.6 8.3 %all_gather.15 = bf16[1,512,768]{1,2,0:T(8,128)(2,1)S(1)} all-gather(bf16[1,512,192]{1,2,0:T(8,128)(2,1)S(1)} %fusion.98), channel_id=1, replica_groups=mesh['dp'=4,'seq'=2,'mp'=4] {'mp'}, dimensions={2}, use_global_device_ids=true | all-gather | bytes 983040 | tf_op jit(solution)/shard_map/all_gather | solution.py:246
  185.9 2.1 convolution_bitcast_fusion.3
  192.3 3.4 collective-permute-start.2
  198.3 4.1 collective-permute-done.3
  206.4 2.9 fusion.6
  209.4 4.8 copy.86
  214.2 2.5 copy.151
  216.8 2.8 fusion.5
  219.6 4.8 copy.88
  224.4 2.5 copy.150
  227.0 160.3 %all-reduce.23.cloned.1.call-done = (f32[768,3,192]{0,2,1:T(8,128)}, f32[192,768]{1,0:T(8,128)}, f32[768,2,288]{0,2,1:T(8,128)}, f32[288,768]{1,0:T(8,128)}) async-done(((f32[768,3,192]{0,2,1:T(8,128)}, f32[192,768]{1,0:T(8,128)}, f32[768,2,288]{0,2,1:T(8,128)}, f32[288,768]{1,0:T(8,128)}), (f32[768,3,192]{0,2,1:T(8,128)}, f32[192,768]{1,0:T(8,128)}, f32[768,2,288]{0,2,1:T(8,128)}, ...) | async-done | bytes 5013520 | tf_op jit(solution)/shard_map/psum | solution.py:308
  388.8 23.1 %reduce-scatter.7.cloned.1.call-done = bf16[192,512]{1,0:T(8,128)(2,1)} async-done(((bf16[768,512]{1,0:T(8,128)(2,1)}), bf16[192,512]{1,0:T(8,128)(2,1)}) %reduce-scatter.7.cloned.1.call-update) | async-done | bytes 196624
  414.1 23.5 %reduce-scatter.9.cloned.1.call-done = bf16[192,512]{1,0:T(8,128)(2,1)} async-done(((bf16[768,512]{1,0:T(8,128)(2,1)}), bf16[192,512]{1,0:T(8,128)(2,1)}) %reduce-scatter.9.cloned.1.call-update) | async-done | bytes 196624
  439.9 11.7 %all-reduce.10 = (f32[192]{0:T(256)S(1)}, f32[192]{0:T(256)S(1)}) all-reduce(f32[192]{0:T(256)S(1)} %get-tuple-element.34, f32[192]{0:T(256)S(1)} %get-tuple-element.32), channel_id=1, replica_groups=mesh['dp'=4,'seq'=2,'mp'=4] {'dp'}, use_global_device_ids=true, to_apply=%region_28.29 | all-reduce | flops 384 | bytes 3072 | tf_op jit(solution)/shard_map/psum | solution.py:308
  451.5 5.7 all-reduce.12
  457.2 6.0 %all-reduce.8 = (f32[1,512,1]{1,2,0:T(1,128)S(1)}, f32[1,512,1]{1,2,0:T(1,128)S(1)}) all-reduce(f32[1,512,1]{1,2,0:T(1,128)S(1)} %bitcast.299, f32[1,512,1]{1,2,0:T(1,128)S(1)} %bitcast.300), channel_id=1, replica_groups=mesh['dp'=4,'seq'=2,'mp'=4] {'mp'}, use_global_device_ids=true, to_apply=%region_18.19 | all-reduce | flops 1024 | bytes 8192 | tf_op jit(solution)/shard_map/psum | solution.py:289
  463.3 2.0 fusion.35
  465.3 100.6 %all-reduce.25.cloned.1.call-done = (f32[768,3,192]{0,2,1:T(8,128)}, f32[192,768]{1,0:T(8,128)}, f32[768,2,288]{0,2,1:T(8,128)}, f32[288,768]{1,0:T(8,128)}) async-done(((f32[768,3,192]{0,2,1:T(8,128)}, f32[192,768]{1,0:T(8,128)}, f32[768,2,288]{0,2,1:T(8,128)}, f32[288,768]{1,0:T(8,128)}), (f32[768,3,192]{0,2,1:T(8,128)}, f32[192,768]{1,0:T(8,128)}, f32[768,2,288]{0,2,1:T(8,128)}, ...) | async-done | bytes 5013520 | tf_op jit(solution)/shard_map/psum | solution.py:307
  566.0 2.9 copy.162
  (215 shorter events, 52.2 us)
Async XLA Ops:
  7.2 10.9 %copy-start = (bf16[768,3,192]{0,2,1:T(8,128)(2,1)S(1)}, bf16[768,3,192]{0,2,1:T(8,128)(2,1)}, u32[]{:S(2)}) copy-start(bf16[768,3,192]{0,2,1:T(8,128)(2,1)} %param.12) | copy-start | bytes 2654212
  7.2 10.9 %copy-start.43 = (f32[768]{0:T(1024)S(1)}, f32[768]{0:T(1024)}, u32[]{:S(2)}) copy-start(f32[768]{0:T(1024)} %param.10) | copy-start | bytes 9220
  7.2 77.0 %all-reduce.19.cloned.1.call-start = ((), (), s32[]{:S(2)}) async-start(), calls=%async_computation.5 | async-start | bytes 3145728
  22.8 7.3 %collective-permute-start = (bf16[1,64,384]{1,2,0:T(8,128)(2,1)}, bf16[1,64,384]{1,2,0:T(8,128)(2,1)}, u32[]{:S(2)}, u32[]{:S(2)}) collective-permute-start(bf16[1,64,384]{1,2,0:T(8,128)(2,1)} %get-tuple-element.77), channel_id=1, source_target_pairs={{0,4},{1,5},{2,6},{3,7},{8,12},{9,13},{10,14},{11,15},{16,20},{17,... | collective-permute-start | bytes 147464 | tf_op jit(solution)/shard_map/ppermute | solution.py:16
  26.9 7.0 %collective-permute-start.1 = (bf16[1,64,384]{1,2,0:T(8,128)(2,1)}, bf16[1,64,384]{1,2,0:T(8,128)(2,1)}, u32[]{:S(2)}, u32[]{:S(2)}) collective-permute-start(bf16[1,64,384]{1,2,0:T(8,128)(2,1)} %get-tuple-element.78), channel_id=1, source_target_pairs={{4,0},{5,1},{6,2},{7,3},{12,8},{13,9},{14,10},{15,11},{20,16},{21,... | collective-permute-start | bytes 147464 | tf_op jit(solution)/shard_map/ppermute | solution.py:19
  30.0 5.4 copy-start.22
  41.3 42.9 %copy-start.33 = (bf16[1,512,192]{1,2,0:T(8,128)(2,1)S(1)}, bf16[1,512,192]{1,2,0:T(8,128)(2,1)}, u32[]{:S(2)}) copy-start(bf16[1,512,192]{1,2,0:T(8,128)(2,1)} %param.8) | copy-start | bytes 589828
  41.3 45.1 %copy-start.10 = (bf16[1,512,192]{1,2,0:T(8,128)(2,1)S(1)}, bf16[1,512,192]{1,2,0:T(8,128)(2,1)}, u32[]{:S(2)}) copy-start(bf16[1,512,192]{1,2,0:T(8,128)(2,1)} %param.9) | copy-start | bytes 589828
  41.3 64.9 %all-gather.2.cloned.1.call-start = ((), (), s32[]{:S(2)}) async-start(), calls=%async_computation.2 | async-start | bytes 1966080 | tf_op jit(solution)/shard_map/all_gather | solution.py:204
  86.4 77.8 %all-reduce.21.cloned.1.call-start = ((), (), s32[]{:S(2)}) async-start(), calls=%async_computation.6 | async-start | bytes 3145728
  106.3 2.4 copy-start.3
  121.2 266.1 %all-reduce.23.cloned.1.call-start = ((), (), s32[]{:S(2)}) async-start(), calls=%async_computation.7 | async-start | bytes 10027008 | tf_op jit(solution)/shard_map/psum | solution.py:308
  121.2 3.9 copy-start.39
  121.2 3.9 copy-start.41
  127.0 45.3 %copy-start.11 = (bf16[1,512,192]{1,2,0:T(8,128)(2,1)S(1)}, bf16[1,512,192]{1,2,0:T(8,128)(2,1)}, u32[]{:S(2)}) copy-start(bf16[1,512,192]{1,2,0:T(8,128)(2,1)} %param.9) | copy-start | bytes 589828
  172.3 9.6 %copy-start.19 = (bf16[192,768]{1,0:T(8,128)(2,1)S(1)}, bf16[192,768]{1,0:T(8,128)(2,1)}, u32[]{:S(2)}) copy-start(bf16[192,768]{1,0:T(8,128)(2,1)} %param.13) | copy-start | bytes 884740
  172.3 9.9 %copy-start.14 = (bf16[1,4,128,3,64]{2,1,4,3,0:T(4,128)(2,1)S(1)}, bf16[1,4,128,3,64]{2,1,4,3,0:T(4,128)(2,1)}, u32[]{:S(2)}) copy-start(bf16[1,4,128,3,64]{2,1,4,3,0:T(4,128)(2,1)} %copy-done.13) | copy-start | bytes 589828
  184.2 3.8 copy-start.24
  185.9 2.2 copy-start.2
  185.9 2.2 copy-start.30
  185.9 2.2 copy-start.32
  192.3 5.9 %collective-permute-start.2 = (bf16[1,64,384]{1,2,0:T(8,128)(2,1)S(1)}, bf16[1,64,384]{1,2,0:T(8,128)(2,1)S(1)}, u32[]{:S(2)}, u32[]{:S(2)}) collective-permute-start(bf16[1,64,384]{1,2,0:T(8,128)(2,1)S(1)} %get-tuple-element.59), channel_id=1, source_target_pairs={{0,4},{1,5},{2,6},{3,7},{8,12},{9,13},{10,14},{11,15},{16,20},{17,... | collective-permute-start | bytes 147464 | tf_op jit(solution)/shard_map/ppermute | solution.py:16
  195.7 6.7 %collective-permute-start.3 = (bf16[1,64,384]{1,2,0:T(8,128)(2,1)S(1)}, bf16[1,64,384]{1,2,0:T(8,128)(2,1)S(1)}, u32[]{:S(2)}, u32[]{:S(2)}) collective-permute-start(bf16[1,64,384]{1,2,0:T(8,128)(2,1)S(1)} %get-tuple-element.60), channel_id=1, source_target_pairs={{4,0},{5,1},{6,2},{7,3},{12,8},{13,9},{14,10},{15,11},{20,16},{21,... | collective-permute-start | bytes 147464 | tf_op jit(solution)/shard_map/ppermute | solution.py:19
  204.3 2.1 copy-start.34
  204.3 2.1 copy-start.35
  206.4 205.5 %reduce-scatter.7.cloned.1.call-start = ((), (), s32[]{:S(2)}) async-start(), calls=%async_computation.3 | async-start | bytes 983040
  216.7 220.8 %reduce-scatter.9.cloned.1.call-start = ((), (), s32[]{:S(2)}) async-start(), calls=%async_computation.4 | async-start | bytes 983040
  226.9 339.0 %all-reduce.25.cloned.1.call-start = ((), (), s32[]{:S(2)}) async-start(), calls=%async_computation.8 | async-start | bytes 10027008 | tf_op jit(solution)/shard_map/psum | solution.py:307
  388.8 74.5 %copy-start.6 = (f32[1,512,192]{1,0,2:T(1,128)S(1)}, f32[1,512,192]{1,0,2:T(1,128)}, u32[]{:S(2)}) copy-start(f32[1,512,192]{1,0,2:T(1,128)} %copy-done.5) | copy-start | bytes 1179652
  388.8 74.5 %copy-start.12 = (bf16[1,512,192]{1,2,0:T(8,128)(2,1)S(1)}, bf16[1,512,192]{1,2,0:T(8,128)(2,1)}, u32[]{:S(2)}) copy-start(bf16[1,512,192]{1,2,0:T(8,128)(2,1)} %param.9) | copy-start | bytes 589828
  566.0 3.0 copy-start.36
  566.0 3.8 copy-start.9
  (25 other events, 26.3 us)
Sparse Core Ops, SparseCore 0:
  41.5 42.7 all-reduce.18
  86.5 19.6 all-gather.1
  121.3 42.8 all-reduce.20
  206.5 180.7 all-reduce.22
  389.7 22.1 reduce-scatter.6
  414.3 23.2 reduce-scatter.8
  440.2 125.7 all-reduce.24
